TPU v7x, 32 devices: a whole 2x2x4 slice. The times are simulated.
32 devices in a mesh: expert: 8 (over y, x, core), tensor: 4 (over z).
Axes of the slice: x: 2, y: 2, z: 4, core: 2. Of those that a mesh axis runs over, the one named last changes fastest.
Arguments:
- tokens: bfloat16 [8192, 1024], P('expert'), may hold values from -6 to 6
- cotangent: bfloat16 [8192, 1024], P('expert'), may hold values from -6 to 6
- routes: int32 [8192], P('expert'), may hold values from 0 to 15, as said below
- slot_index: int32 [8192], P('expert'), may hold values from 0 to 128, as said below
- first_gain: float32 [1024], replicated, may hold values from 0.1 to 1.9
- first_shift: float32 [1024], replicated, may hold values from -1.25 to 1.25
- project_in: bfloat16 [1024, 3, 1024], P(None, None, 'tensor'), may hold values from -0.25 to 0.25
- project_out: bfloat16 [1024, 1024], P('tensor'), may hold values from -1.5 to 1.5
- second_gain: float32 [1024], replicated, may hold values from 0.1 to 1.9
- second_shift: float32 [1024], replicated, may hold values from -1.25 to 1.25
- router_weight: bfloat16 [1024, 16], replicated, may hold values from -0.09375 to 0.09375
- mixing_weight: bfloat16 [1024, 2], replicated, may hold values from -0.1875 to 0.1875
- dense_up: bfloat16 [1024, 4096], P(None, 'tensor'), may hold values from -0.1875 to 0.1875
- dense_down: bfloat16 [4096, 1024], P('tensor'), may hold values from -0.1875 to 0.1875
- expert_up: bfloat16 [16, 1024, 4096], P('expert', None, 'tensor'), may hold values from -0.375 to 0.375
- expert_down: bfloat16 [16, 4096, 1024], P('expert', 'tensor'), may hold values from -3 to 3
Outputs:
- layer_out: bfloat16 [8192, 1024], P('expert')
- input_grad: bfloat16 [8192, 1024], P('expert')
- first_gain_grad: float32 [1024], replicated
- first_shift_grad: float32 [1024], replicated
- project_in_grad: float32 [1024, 3, 1024], P(None, None, 'tensor')
- project_out_grad: float32 [1024, 1024], P('tensor')
- second_gain_grad: float32 [1024], replicated
- second_shift_grad: float32 [1024], replicated
- router_grad: float32 [1024, 16], replicated
- mixing_grad: float32 [1024, 2], replicated
- dense_up_grad: float32 [1024, 4096], P(None, 'tensor')
- dense_down_grad: float32 [4096, 1024], P('tensor')
- expert_up_grad: float32 [16, 1024, 4096], P('expert', None, 'tensor')
- expert_down_grad: float32 [16, 4096, 1024], P('expert', 'tensor')
Inputs may be any that keep to these rules, and one draw needn't show every extreme that they name: `routes`: in every block of 1024 tokens (tokens b * 1024 to (b + 1) * 1024 - 1) some expert is named by more than 128 tokens. slot_index[t] is the number of earlier tokens of t's block with the same route, or 128 where that number is 128 or more (the token is dropped); so at most 128 kept tokens of a block name one expert, and every block fills all 128 slots of some expert.
All inputs are finite; a program needn't handle non-finite values.
Results may differ from a plain program's by a relative error of at most 0.023.
Values may be sent and summed in bfloat16 or wider, within the bound.
No kernel may reach another device: no remote copies, remote signals or barrier semaphores. Data moves between devices by JAX's collectives and lax.ppermute only.
A program may use at most 192 MiB of HBM per device.

v0:
```python
import jax
import jax.numpy as jnp
from jax import lax
from jax.sharding import PartitionSpec as P

HEAD_DIM = 64
SEQ = 1024
EPS = 1e-05
NEGATIVE = -1e30


def layer_norm(row_values, norm_gain, norm_shift):
    row_mean = jnp.mean(row_values, axis=-1, keepdims=True)
    centred = row_values - row_mean
    spread = jnp.mean(centred * centred, axis=-1, keepdims=True)
    return centred * lax.rsqrt(spread + EPS) * norm_gain + norm_shift


def gelu_tanh(values):
    return jax.nn.gelu(values, approximate=True)


def gelu_back(pre_act, incoming):
    return jax.vjp(gelu_tanh, pre_act)[1](incoming)[0]


def causal_scores(query_block, key_seq, offset):
    score_scale = HEAD_DIM ** (-0.5)
    scores = (
        jnp.einsum("qhd,khd->hqk", query_block, key_seq, preferred_element_type=jnp.float32)
        * score_scale
    )
    query_pos = offset + lax.iota(jnp.int32, query_block.shape[0])
    key_pos = lax.iota(jnp.int32, key_seq.shape[0])
    allowed = key_pos[None, :] <= query_pos[:, None]
    return jnp.where(allowed[None], scores, NEGATIVE)


def attend_forward(queries, key_rows, values, block_rows):
    row_count, head_count, head_width = queries.shape
    per_seq = SEQ // block_rows

    def one_block(block_index):
        seq_start = block_index // per_seq * SEQ
        offset = block_index % per_seq * block_rows
        query_block = lax.dynamic_slice_in_dim(queries, seq_start + offset, block_rows, 0)
        scores = causal_scores(query_block, key_rows, offset)
        row_max = jnp.max(scores, axis=-1, keepdims=True)
        powers = jnp.exp(scores - row_max)
        row_total = jnp.sum(powers, axis=-1, keepdims=True)
        weights = (powers / row_total).astype(jnp.bfloat16)
        blended = jnp.einsum("hqk,khd->qhd", weights, values, preferred_element_type=jnp.float32)
        return (blended.astype(jnp.bfloat16), (row_max + jnp.log(row_total))[..., 0])

    blended, log_total = lax.map(one_block, jnp.arange(row_count // block_rows, dtype=jnp.int32))
    return (blended.reshape(row_count, head_count * head_width), log_total)


def attend_backward(queries, key_rows, values, log_total, grad_blended, block_rows):
    row_count, head_count, head_width = queries.shape
    per_seq = SEQ // block_rows
    score_scale = HEAD_DIM ** (-0.5)

    def one_seq(sequence):
        seq_start = sequence * SEQ

        def step(totals, inner_index):
            key_acc, value_acc = totals
            offset = inner_index * block_rows
            query_block = lax.dynamic_slice_in_dim(queries, seq_start + offset, block_rows, 0)
            grad_block = lax.dynamic_slice_in_dim(grad_blended, seq_start + offset, block_rows, 0)
            row_log = lax.dynamic_index_in_dim(
                log_total, sequence * per_seq + inner_index, 0, keepdims=False
            )
            scores = causal_scores(query_block, key_rows, offset)
            weights = jnp.exp(scores - row_log[..., None])
            weight_grad = jnp.einsum(
                "qhd,khd->hqk", grad_block, values, preferred_element_type=jnp.float32
            )
            row_inner = jnp.sum(weights * weight_grad, axis=-1, keepdims=True)
            score_grad = (weights * (weight_grad - row_inner)).astype(jnp.bfloat16)
            query_grad = (
                jnp.einsum("hqk,khd->qhd", score_grad, key_rows, preferred_element_type=jnp.float32)
                * score_scale
            )
            key_acc = (
                key_acc
                + jnp.einsum(
                    "hqk,qhd->khd", score_grad, query_block, preferred_element_type=jnp.float32
                )
                * score_scale
            )
            value_acc = value_acc + jnp.einsum(
                "hqk,qhd->khd",
                weights.astype(jnp.bfloat16),
                grad_block,
                preferred_element_type=jnp.float32,
            )
            return ((key_acc, value_acc), query_grad)

        empty_acc = jnp.zeros((SEQ, head_count, head_width), jnp.float32)
        (key_grad, value_grad), query_grad = lax.scan(
            step, (empty_acc, empty_acc), jnp.arange(per_seq, dtype=jnp.int32)
        )
        return (query_grad.reshape(SEQ, head_count, head_width), key_grad, value_grad)

    query_grad, key_grad, value_grad = lax.map(
        one_seq, jnp.arange(row_count // SEQ, dtype=jnp.int32)
    )
    flat_width = head_count * head_width
    return jnp.stack(
        [
            query_grad.reshape(row_count, flat_width),
            key_grad.reshape(row_count, flat_width),
            value_grad.reshape(row_count, flat_width),
        ],
        axis=1,
    )


def send_home(buffer):
    return lax.all_to_all(
        buffer.astype(jnp.bfloat16), "expert", split_axis=1, concat_axis=0, tiled=True
    ).astype(buffer.dtype)


def send_grads_home(buffer):
    return lax.all_to_all(
        buffer.astype(jnp.bfloat16), "expert", split_axis=1, concat_axis=0, tiled=True
    ).astype(buffer.dtype)


def local(
    tokens,
    cotangent,
    routes,
    slot_index,
    first_gain,
    first_shift,
    project_in,
    project_out,
    second_gain,
    second_shift,
    router_weight,
    mixing_weight,
    dense_up,
    dense_down,
    expert_up,
    expert_down,
):
    inputs = tokens.astype(jnp.float32)
    cotan_rows = cotangent.astype(jnp.float32)
    row_count, model_width = inputs.shape
    expert_count = router_weight.shape[1]
    capacity = 2 * row_count // expert_count
    head_count = project_in.shape[2] // HEAD_DIM
    block_rows = min(512, SEQ)
    normed_in, first_back = jax.vjp(layer_norm, inputs, first_gain, first_shift)
    normed_low = normed_in.astype(jnp.bfloat16)
    projected = jnp.einsum(
        "td,dcn->tcn", normed_low, project_in, preferred_element_type=jnp.float32
    ).astype(jnp.bfloat16)
    queries = projected[:, 0].reshape(row_count, head_count, HEAD_DIM)
    key_rows = projected[:, 1].reshape(row_count, head_count, HEAD_DIM)
    values = projected[:, 2].reshape(row_count, head_count, HEAD_DIM)
    attended, log_total = attend_forward(queries, key_rows, values, block_rows)
    attn_part = jnp.dot(attended, project_out, preferred_element_type=jnp.float32)
    attn_full = lax.psum(attn_part, "tensor")
    residual = inputs + attn_full
    normed_mid, second_back = jax.vjp(layer_norm, residual, second_gain, second_shift)
    mid_low = normed_mid.astype(jnp.bfloat16)
    router_logits = jnp.dot(mid_low, router_weight, preferred_element_type=jnp.float32)
    mixing_logits = jnp.dot(mid_low, mixing_weight, preferred_element_type=jnp.float32)
    chosen = routes[:, None] == lax.iota(jnp.int32, expert_count)[None, :]

    def gating(route_logits, mix_logits):
        router_probs = jax.nn.softmax(route_logits, axis=-1)
        return (
            jnp.sum(jnp.where(chosen, router_probs, 0.0), axis=-1),
            jax.nn.softmax(mix_logits, axis=-1),
        )

    (gate_value, mixing), gating_back = jax.vjp(gating, router_logits, mixing_logits)
    slot_total = expert_count * capacity
    slot_place = jnp.where(slot_index < capacity, routes * capacity + slot_index, slot_total)
    holder = (
        jnp.full((slot_total,), row_count, jnp.int32)
        .at[slot_place]
        .set(lax.iota(jnp.int32, row_count), mode="drop")
    )

    def to_slots(row_values):
        taken = jnp.take(row_values, holder, axis=0, mode="fill", fill_value=0)
        return taken.reshape(expert_count, capacity, row_values.shape[1])

    def from_slots(buffer):
        return jnp.take(
            buffer.reshape(slot_total, buffer.shape[-1]),
            slot_place,
            axis=0,
            mode="fill",
            fill_value=0,
        )

    arrived = lax.all_to_all(to_slots(mid_low), "expert", split_axis=0, concat_axis=1, tiled=True)
    expert_pre = jnp.einsum("erd,edf->erf", arrived, expert_up, preferred_element_type=jnp.float32)
    expert_hidden = gelu_tanh(expert_pre).astype(jnp.bfloat16)
    expert_part = jnp.einsum(
        "erf,efd->erd", expert_hidden, expert_down, preferred_element_type=jnp.float32
    )
    dense_pre = jnp.dot(mid_low, dense_up, preferred_element_type=jnp.float32)
    dense_hidden = gelu_tanh(dense_pre).astype(jnp.bfloat16)
    dense_part = jnp.dot(dense_hidden, dense_down, preferred_element_type=jnp.float32)
    dense_weight = mixing[:, 0:1]
    expert_weight = (mixing[:, 1] * gate_value)[:, None]
    dense_full, expert_full = (
        lax.psum(dense_part.astype(jnp.bfloat16), "tensor").astype(jnp.float32),
        lax.psum(expert_part.astype(jnp.bfloat16), "tensor").astype(jnp.float32),
    )
    expert_tok = from_slots(send_home(expert_full))
    layer_out = residual + dense_weight * dense_full + expert_weight * expert_tok
    dense_dot = jnp.sum(cotan_rows * dense_full, axis=-1)
    expert_dot = jnp.sum(cotan_rows * expert_tok, axis=-1)
    dense_out_grad = (cotan_rows * dense_weight).astype(jnp.bfloat16)
    expert_tok_grad = (cotan_rows * expert_weight).astype(jnp.bfloat16)
    mixing_dots = jnp.stack([dense_dot, gate_value * expert_dot], axis=-1)
    gate_grad = mixing[:, 1] * expert_dot
    router_logit_grad, mixing_logit_grad = gating_back((gate_grad, mixing_dots))
    router_low = router_logit_grad.astype(jnp.bfloat16)
    mixing_low = mixing_logit_grad.astype(jnp.bfloat16)
    router_grad = jnp.einsum("td,te->de", mid_low, router_low, preferred_element_type=jnp.float32)
    mixing_grad = jnp.einsum("td,te->de", mid_low, mixing_low, preferred_element_type=jnp.float32)
    mid_from_gates = jnp.einsum(
        "te,de->td", router_low, router_weight, preferred_element_type=jnp.float32
    ) + jnp.einsum("te,de->td", mixing_low, mixing_weight, preferred_element_type=jnp.float32)
    dense_down_grad = jnp.einsum(
        "tf,td->fd", dense_hidden, dense_out_grad, preferred_element_type=jnp.float32
    )
    dense_hidden_grad = jnp.einsum(
        "td,fd->tf", dense_out_grad, dense_down, preferred_element_type=jnp.float32
    )
    dense_pre_grad = gelu_back(dense_pre, dense_hidden_grad).astype(jnp.bfloat16)
    dense_up_grad = jnp.einsum(
        "td,tf->df", mid_low, dense_pre_grad, preferred_element_type=jnp.float32
    )
    mid_dense_part = jnp.einsum(
        "tf,df->td", dense_pre_grad, dense_up, preferred_element_type=jnp.float32
    )
    grad_arrived = lax.all_to_all(
        to_slots(expert_tok_grad), "expert", split_axis=0, concat_axis=1, tiled=True
    )
    expert_down_grad = jnp.einsum(
        "erf,erd->efd", expert_hidden, grad_arrived, preferred_element_type=jnp.float32
    )
    expert_hidden_grad = jnp.einsum(
        "erd,efd->erf", grad_arrived, expert_down, preferred_element_type=jnp.float32
    )
    expert_pre_grad = gelu_back(expert_pre, expert_hidden_grad).astype(jnp.bfloat16)
    expert_up_grad = jnp.einsum(
        "erd,erf->edf", arrived, expert_pre_grad, preferred_element_type=jnp.float32
    )
    arrived_grad = jnp.einsum(
        "erf,edf->erd", expert_pre_grad, expert_up, preferred_element_type=jnp.float32
    )
    mid_dense, arrived_full = (
        lax.psum(mid_dense_part.astype(jnp.bfloat16), "tensor").astype(jnp.float32),
        lax.psum(arrived_grad.astype(jnp.bfloat16), "tensor").astype(jnp.float32),
    )
    mid_grad = mid_dense + from_slots(send_grads_home(arrived_full)) + mid_from_gates
    resid_from_mid, second_gain_grad, second_shift_grad = second_back(mid_grad)
    residual_grad = cotan_rows + resid_from_mid
    attn_grad_low = residual_grad.astype(jnp.bfloat16)
    project_out_grad = jnp.einsum(
        "tn,td->nd", attended, attn_grad_low, preferred_element_type=jnp.float32
    )
    attended_grad = jnp.einsum(
        "td,nd->tn", attn_grad_low, project_out, preferred_element_type=jnp.float32
    ).astype(jnp.bfloat16)
    qkv_grad = attend_backward(
        queries,
        key_rows,
        values,
        log_total,
        attended_grad.reshape(row_count, head_count, HEAD_DIM),
        block_rows,
    ).astype(jnp.bfloat16)
    project_in_grad = jnp.einsum(
        "td,tcn->dcn", normed_low, qkv_grad, preferred_element_type=jnp.float32
    )
    normed_part = jnp.einsum(
        "tcn,dcn->td", qkv_grad, project_in, preferred_element_type=jnp.float32
    )
    normed_grad = lax.psum(normed_part.astype(jnp.bfloat16), "tensor").astype(jnp.float32)
    input_from_norm, first_gain_grad, first_shift_grad = first_back(normed_grad)
    input_grad = (residual_grad + input_from_norm).astype(jnp.bfloat16)
    (
        router_grad,
        mixing_grad,
        dense_up_grad,
        dense_down_grad,
        second_gain_grad,
        second_shift_grad,
        project_out_grad,
        project_in_grad,
        first_gain_grad,
        first_shift_grad,
    ) = (
        lax.psum(router_grad.astype(jnp.bfloat16), "expert").astype(jnp.float32),
        lax.psum(mixing_grad.astype(jnp.bfloat16), "expert").astype(jnp.float32),
        lax.psum(dense_up_grad.astype(jnp.bfloat16), "expert").astype(jnp.float32),
        lax.psum(dense_down_grad.astype(jnp.bfloat16), "expert").astype(jnp.float32),
        lax.psum(second_gain_grad.astype(jnp.bfloat16), "expert").astype(jnp.float32),
        lax.psum(second_shift_grad.astype(jnp.bfloat16), "expert").astype(jnp.float32),
        lax.psum(project_out_grad.astype(jnp.bfloat16), "expert").astype(jnp.float32),
        lax.psum(project_in_grad.astype(jnp.bfloat16), "expert").astype(jnp.float32),
        lax.psum(first_gain_grad.astype(jnp.bfloat16), "expert").astype(jnp.float32),
        lax.psum(first_shift_grad.astype(jnp.bfloat16), "expert").astype(jnp.float32),
    )
    return (
        layer_out.astype(jnp.bfloat16),
        input_grad,
        first_gain_grad,
        first_shift_grad,
        project_in_grad,
        project_out_grad,
        second_gain_grad,
        second_shift_grad,
        router_grad,
        mixing_grad,
        dense_up_grad,
        dense_down_grad,
        expert_up_grad,
        expert_down_grad,
    )


def solution(mesh):
    placed = (
        P("expert", None),
        P("expert", None),
        P("expert"),
        P("expert"),
        P(),
        P(),
        P(None, None, "tensor"),
        P("tensor", None),
        P(),
        P(),
        P(),
        P(),
        P(None, "tensor"),
        P("tensor", None),
        P("expert", None, "tensor"),
        P("expert", "tensor", None),
    )
    return jax.shard_map(
        local,
        mesh=mesh,
        in_specs=placed,
        out_specs=(
            P("expert", None),
            P("expert", None),
            P(),
            P(),
            P(None, None, "tensor"),
            P("tensor", None),
            P(),
            P(),
            P(),
            P(),
            P(None, "tensor"),
            P("tensor", None),
            P("expert", None, "tensor"),
            P("expert", "tensor", None),
        ),
        check_vma=False,
    )
```

profile of v0, /device:TPU:0, one launch (start us, length us, event | category | flops | bytes accessed | tf_op | source)
XLA Modules:
  0.0 1272.1 jit_solution(15387023293925295045)
XLA Ops:
  16.1 23.0 %while.43 = (s32[]{:T(128)}, bf16[2,512,4,64]{1,3,2,0:T(8,128)(2,1)}, f32[2,4,512]{2,1,0:T(4,128)S(1)}, s32[2]{0:T(128)S(1)}, bf16[1024,4,64]{0,2,1:T(8,128)(2,1...) while((s32[]{:T(128)}, ...), condition=%wide.region_5.6_spmd, body=%wide.region_2.5_spmd.sunk | while | flops 562690560 | bytes 35197428 | solution.py:55
  23.7 3.0 fusion.171
  35.2 3.0 fusion.171
  41.9 3.8 fusion.104
  46.4 4.5 scatter_custom_fusion
  50.9 152.7 %all-reduce.10.cloned.1.call-done = f32[1024,1024]{1,0:T(8,128)} async-done(((f32[1024,1024]{1,0:T(8,128)}), f32[1024,1024]{1,0:T(8,128)}) %all-reduce.10.cloned.1.call-update) | async-done | bytes 4194320 | tf_op jit(solution)/shard_map/psum | solution.py:168
  203.6 3.3 fusion.99
  211.6 12.8 %gather_fusion = bf16[2048,1024]{1,0:T(8,128)(2,1)} fusion(bf16[1024,1024]{1,0:T(8,128)(2,1)} %add_convert_fusion.1, s32[2048]{0:T(1024)S(1)} %fusion.86), kind=kCustom, calls=%fused_computation.clone | custom fusion | bytes 8396800 | tf_op jit(solution)/shard_map/jit(_take)/gather | solution.py:193
  224.4 3.8 broadcast_select_fusion.1
  228.2 4.6 all-to-all-start
  232.8 4.6 fusion.105
  239.4 4.0 convolution_convert_fusion.5
  243.4 38.5 %all-to-all-done = bf16[16,128,1024]{2,1,0:T(8,128)(2,1)} async-done(((bf16[16,128,1024]{2,1,0:T(8,128)(2,1)}), bf16[16,128,1024]{2,1,0:T(8,128)(2,1)}, u32[]{:S(2)}, u32[]{:S(2)}) %all-to-all-start) | async-done | bytes 4194336 | tf_op jit(solution)/shard_map/all_to_all | solution.py:205
  281.9 2.8 copy.54
  286.7 4.5 fusion.106
  291.2 3.4 copy-done.81
  294.6 6.8 convolution_convert_fusion.1
  301.4 220.2 %all-reduce.18.cloned.1.call-done = (bf16[1024,1024]{1,0:T(8,128)(2,1)}, bf16[2,1024,1024]{2,1,0:T(8,128)(2,1)}) async-done(((bf16[1024,1024]{1,0:T(8,128)(2,1)}, bf16[2,1024,1024]{2,1,0:T(8,128)(2,1)}), (bf16[1024,1024]{1,0:T(8,128)(2,1)}, bf16[2,1024,1024]{2,1,0:T(8,128)(2,1)})) %all-reduce.18.cloned.1.call-update) | async-done | bytes 6291472 | tf_op jit(solution)/shard_map/psum | solution.py:217
  521.6 8.5 copy.55
  530.2 4.7 all-to-all-start.1
  539.6 44.4 %all-to-all-done.1 = bf16[2,1024,1024]{2,0,1:T(2,128)(2,1)} async-done(((bf16[2,1024,1024]{2,0,1:T(2,128)(2,1)}), bf16[2,1024,1024]{2,0,1:T(2,128)(2,1)}, u32[]{:S(2)}, u32[]{:S(2)}) %all-to-all-start.1) | async-done | bytes 4194336 | tf_op jit(solution)/shard_map/all_to_all | solution.py:122
  584.0 7.1 copy.56
  591.1 9.7 gather_fusion.1
  600.8 4.5 fusion.68
  607.2 12.8 %gather_fusion.2 = bf16[2048,1024]{1,0:T(8,128)(2,1)} fusion(bf16[1024,1024]{1,0:T(8,128)(2,1)} %fusion.66, s32[2048]{0:T(1024)S(1)} %fusion.86), kind=kCustom, calls=%fused_computation.2.clone | custom fusion | bytes 8396800 | tf_op jit(solution)/shard_map/jit(_take)/gather | solution.py:193
  620.0 3.8 broadcast_select_fusion
  623.8 4.6 all-to-all-start.2
  628.5 7.7 fusion.62
  637.6 3.7 convolution_convert_fusion.4
  641.3 36.3 %all-to-all-done.2 = bf16[16,128,1024]{2,1,0:T(8,128)(2,1)} async-done(((bf16[16,128,1024]{2,1,0:T(8,128)(2,1)}), bf16[16,128,1024]{2,1,0:T(8,128)(2,1)}, u32[]{:S(2)}, u32[]{:S(2)}) %all-to-all-start.2) | async-done | bytes 4194336 | tf_op jit(solution)/shard_map/all_to_all | solution.py:249
  677.5 2.8 copy.57
  681.0 12.1 fusion.43
  695.1 6.2 convolution_convert_fusion
  701.3 220.1 %all-reduce.16.cloned.1.call-done = (bf16[2,1024,1024]{2,1,0:T(8,128)(2,1)}, bf16[1024,1024]{1,0:T(8,128)(2,1)}) async-done(((bf16[2,1024,1024]{2,1,0:T(8,128)(2,1)}, bf16[1024,1024]{1,0:T(8,128)(2,1)}), (bf16[2,1024,1024]{2,1,0:T(8,128)(2,1)}, bf16[1024,1024]{1,0:T(8,128)(2,1)})) %all-reduce.16.cloned.1.call-update) | async-done | bytes 6291472 | tf_op jit(solution)/shard_map/psum | solution.py:267
  921.5 8.5 copy.58
  930.0 4.7 all-to-all-start.3
  936.8 2.8 fusion.95
  939.6 44.2 %all-to-all-done.3 = bf16[2,1024,1024]{2,0,1:T(2,128)(2,1)} async-done(((bf16[2,1024,1024]{2,0,1:T(2,128)(2,1)}), bf16[2,1024,1024]{2,0,1:T(2,128)(2,1)}, u32[]{:S(2)}, u32[]{:S(2)}) %all-to-all-start.3) | async-done | bytes 4194336 | tf_op jit(solution)/shard_map/all_to_all | solution.py:128
  983.8 7.1 copy.59
  990.9 9.8 gather_fusion.3
  1000.8 7.5 multiply_reduce_fusion.1
  1009.0 3.6 fusion.98
  1016.7 33.2 %while.44 = (s32[]{:T(128)}, f32[1024,4,64]{0,2,1:T(8,128)}, f32[1024,4,64]{0,2,1:T(8,128)}, bf16[2,512,4,64]{1,3,2,0:T(8,128)(2,1)}, s32[2]{0:T(128)S(1)}, /*in...) while((s32[]{:T(128)}, f32[1024,4,64]{0,2,1:T(8,128)}, ...), condition=%wide.region_27.30_spmd.clone, body=%wide.region_25.29_spmd.clone.sunk | while | flops 1375599104 | bytes 97579512 | solution.py:102
  1021.8 2.5 fusion.183
  1024.4 3.2 multiply_reduce_fusion.6
  1027.6 2.4 multiply_convert_fusion.11
  1038.3 2.6 fusion.183
  1040.9 3.2 multiply_reduce_fusion.6
  1044.0 2.4 multiply_convert_fusion.11
  1057.6 4.9 bitcast_convert_fusion
  1063.0 5.5 convolution_convert_fusion.3
  1068.5 4.4 convolution_convert_fusion.2
  1074.5 3.3 convolution_convert_fusion.6
  1077.9 13.6 %fusion.97 = f32[2,1024,1024]{2,1,0:T(8,128)} fusion(bf16[2,1024,1024]{2,1,0:T(8,128)(2,1)} %bitcast.152, f32[2,1024,1024]{2,1,0:T(8,128)} %copy-done.81), kind=kOutput, calls=%fused_computation.170 | convolution fusion | flops 4313841664 | bytes 20971520 | tf_op jit(solution)/shard_map/erf,erd->efd/dot_general | solution.py:252
  1091.5 6.9 fusion.107
  1098.4 47.4 %all-reduce.12.cloned.1.call-done = bf16[1024,1024]{1,0:T(8,128)(2,1)} async-done(((bf16[1024,1024]{1,0:T(8,128)(2,1)}), bf16[1024,1024]{1,0:T(8,128)(2,1)}) %all-reduce.12.cloned.1.call-update) | async-done | bytes 2097168 | tf_op jit(solution)/shard_map/psum | solution.py:293
  1147.9 2.7 fusion.64
  1150.6 2.7 fusion.55
  1153.4 26.6 %all-reduce = (bf16[1024]{0:T(1024)(128)(2,1)S(1)}, bf16[1024]{0:T(1024)(128)(2,1)S(1)}, bf16[1024]{0:T(1024)(128)(2,1)S(1)}, bf16[1024]{0:T(1024)(128)(2,1)S(1)...) all-reduce(bf16[1024]{0:T(1024)(128)(2,1)S(1)} %get-tuple-element.3, ...), channel_id=1, replica_groups=mesh['expert'=8,'tensor'=4] {'expert'}, use_global_device_ids=true, to_apply=%region_32.35 | all-reduce | flops 22528 | bytes 90112 | tf_op jit(solution)/shard_map/psum | solution.py:316
  1183.6 5.5 add_convert_fusion
  1189.1 65.5 %all-reduce.14.cloned.1.call-done = (bf16[1024,3,256]{2,0,1:T(8,128)(2,1)}, bf16[256,1024]{1,0:T(8,128)(2,1)}, bf16[1024,1024]{1,0:T(8,128)(2,1)}, bf16[1024,1024]{1,0:T(8,128)(2,1)}) async-done(((bf16[1024,3,256]{2,0,1:T(8,128)(2,1)}, bf16[256,1024]{1,0:T(8,128)(2,1)}, bf16[1024,1024]{1,0:T(8,128)(2,1)}, bf16[1024,1024]{1,0:T(8,128)(2,1)}), (bf16[1024,3,256]{2,0,1:T(8,128)(2,1)}, ...) | async-done | bytes 6291472 | tf_op jit(solution)/shard_map/psum | solution.py:315
  1256.9 3.3 convert_element_type.230
  1260.3 2.6 convert_element_type.242
  1262.9 2.5 convert_element_type.244
  (289 shorter events, 78.8 us)
Async XLA Ops:
  7.2 232.2 %copy-start = (bf16[1024,1024]{1,0:T(8,128)(2,1)S(1)}, bf16[1024,1024]{1,0:T(8,128)(2,1)}, u32[]{:S(2)}) copy-start(bf16[1024,1024]{1,0:T(8,128)(2,1)} %param.37) | copy-start | bytes 6291460
  7.2 5.8 copy-start.55
  7.2 5.7 copy-start.77
  7.2 196.4 %all-reduce.10.cloned.1.call-start = ((), (), s32[]{:S(2)}) async-start(), calls=%async_computation.4 | async-start | bytes 8388608 | tf_op jit(solution)/shard_map/psum | solution.py:168
  7.3 5.7 copy-start.9
  7.3 5.7 copy-start.76
  9.4 5.8 copy-start.44
  39.0 6.6 copy-start.3
  39.0 6.6 copy-start.11
  39.1 6.6 copy-start.46
  207.6 16.8 %copy-start.63 = (f32[1024]{0:T(1024)}, f32[1024]{0:T(1024)S(1)}, u32[]{:S(2)}) copy-start(f32[1024]{0:T(1024)S(1)} %multiply_reduce_fusion.3) | copy-start | bytes 12292
  228.2 53.7 %all-to-all-start = ((bf16[16,128,1024]{2,1,0:T(8,128)(2,1)}), bf16[16,128,1024]{2,1,0:T(8,128)(2,1)}, u32[]{:S(2)}, u32[]{:S(2)}) async-start(bf16[16,128,1024]{2,1,0:T(8,128)(2,1)} %bitcast.148), calls=%async_computation | async-start | bytes 8388608 | tf_op jit(solution)/shard_map/all_to_all | solution.py:205
  232.8 288.9 %all-reduce.18.cloned.1.call-start = ((), (), s32[]{:S(2)}) async-start(), calls=%async_computation.8 | async-start | bytes 12582912 | tf_op jit(solution)/shard_map/psum | solution.py:217
  281.9 4.8 copy-start.73
  286.7 7.9 copy-start.71
  291.2 3.4 copy-start.81
  530.2 4.8 copy-start.66
  530.2 7.1 copy-start.42
  530.2 53.8 %all-to-all-start.1 = ((bf16[2,1024,1024]{2,0,1:T(2,128)(2,1)}), bf16[2,1024,1024]{2,0,1:T(2,128)(2,1)}, u32[]{:S(2)}, u32[]{:S(2)}) async-start(bf16[2,1024,1024]{2,0,1:T(2,128)(2,1)} %copy.55), calls=%async_computation.1 | async-start | bytes 8388608 | tf_op jit(solution)/shard_map/all_to_all | solution.py:122
  600.8 4.6 copy-start.15
  623.8 53.7 %all-to-all-start.2 = ((bf16[16,128,1024]{2,1,0:T(8,128)(2,1)}), bf16[16,128,1024]{2,1,0:T(8,128)(2,1)}, u32[]{:S(2)}, u32[]{:S(2)}) async-start(bf16[16,128,1024]{2,1,0:T(8,128)(2,1)} %bitcast.147), calls=%async_computation.2 | async-start | bytes 8388608 | tf_op jit(solution)/shard_map/all_to_all | solution.py:249
  628.4 293.0 %all-reduce.16.cloned.1.call-start = ((), (), s32[]{:S(2)}) async-start(), calls=%async_computation.7 | async-start | bytes 12582912 | tf_op jit(solution)/shard_map/psum | solution.py:267
  628.5 9.1 copy-start.75
  677.5 3.4 copy-start.72
  680.4 12.7 copy-start.24
  681.0 14.1 %copy-start.74 = (bf16[2,1024,1024]{2,1,0:T(8,128)(2,1)S(1)}, bf16[2,1024,1024]{2,1,0:T(8,128)(2,1)}, u32[]{:S(2)}) copy-start(bf16[2,1024,1024]{2,1,0:T(8,128)(2,1)} %param.38) | copy-start | bytes 12582916
  930.0 4.8 copy-start.2
  930.0 53.8 %all-to-all-start.3 = ((bf16[2,1024,1024]{2,0,1:T(2,128)(2,1)}), bf16[2,1024,1024]{2,0,1:T(2,128)(2,1)}, u32[]{:S(2)}, u32[]{:S(2)}) async-start(bf16[2,1024,1024]{2,0,1:T(2,128)(2,1)} %copy.58), calls=%async_computation.3 | async-start | bytes 8388608 | tf_op jit(solution)/shard_map/all_to_all | solution.py:128
  934.7 211.2 %all-reduce.12.cloned.1.call-start = ((), (), s32[]{:S(2)}) async-start(), calls=%async_computation.5 | async-start | bytes 4194304 | tf_op jit(solution)/shard_map/psum | solution.py:293
  990.9 9.8 copy-start.49
  990.9 9.8 copy-start.51
  990.9 9.8 copy-start.54
  1000.7 7.6 copy-start.64
  1000.7 7.6 copy-start.6
  1000.7 7.7 copy-start.13
  1000.7 8.3 copy-start.21
  1009.0 3.6 copy-start.16
  1024.4 3.2 copy-start.33
  1040.9 3.2 copy-start.33
  1052.9 4.7 copy-start.37
  1062.5 192.2 %all-reduce.14.cloned.1.call-start = ((), (), s32[]{:S(2)}) async-start(), calls=%async_computation.6 | async-start | bytes 12582912 | tf_op jit(solution)/shard_map/psum | solution.py:315
  1062.9 5.5 copy-start.17
  1062.9 5.5 copy-start.80
  1068.4 4.5 copy-start.26
  1068.4 4.5 copy-start.31
  1068.4 6.0 copy-start.10
  1068.4 6.0 copy-start.38
  1068.4 6.0 copy-start.39
  1068.5 6.0 copy-start.45
  1068.5 6.0 copy-start.56
  1068.5 6.0 copy-start.58
  1068.5 6.0 copy-start.78
  1077.8 13.7 %copy-start.23 = (bf16[2,8,128,1024]{3,2,1,0:T(8,128)(2,1)S(1)}, bf16[2,8,128,1024]{3,2,1,0:T(8,128)(2,1)}, u32[]{:S(2)}) copy-start(bf16[2,8,128,1024]{3,2,1,0:T(8,128)(2,1)} %copy-done.22) | copy-start | bytes 12582916
  1077.9 13.6 %copy-start.83 = (bf16[2,1024,1024]{2,1,0:T(8,128)(2,1)S(1)}, bf16[2,1024,1024]{2,1,0:T(8,128)(2,1)}, u32[]{:S(2)}) copy-start(bf16[2,1024,1024]{2,1,0:T(8,128)(2,1)} %copy-done.82) | copy-start | bytes 12582916
  1098.4 52.2 %copy-start.62 = (f32[1024]{0:T(1024)S(1)}, f32[1024]{0:T(1024)}, u32[]{:S(2)}) copy-start(f32[1024]{0:T(1024)} %copy-done.61) | copy-start | bytes 12292
  1147.8 2.8 copy-start.18
  1147.8 5.5 copy-start.43
  1147.9 5.5 copy-start.65
  1147.9 5.5 copy-start.67
  1147.9 5.5 copy-start.68
  1147.9 35.8 %copy-start.60 = (f32[1024]{0:T(1024)S(1)}, f32[1024]{0:T(1024)}, u32[]{:S(2)}) copy-start(f32[1024]{0:T(1024)} %copy-done.59) | copy-start | bytes 12292
  1254.7 5.6 copy-start.29
  1260.3 2.6 copy-start.28
  1260.3 5.1 copy-start.1
  (41 other events, 66.7 us)
Sparse Core Ops, SparseCore 0:
  45.9 157.6 all-reduce.9
  301.6 220.0 all-reduce.17
  701.5 219.9 all-reduce.15
  1062.6 83.2 all-reduce.11
  1150.5 104.1 all-reduce.13
where the time goes:
time: 1280 us; the launch traced here: 1270 us
  waiting for transfers between devices  869 us (68%)
  matrix products  142 us (11%)
  local copies, waits for them, and re-layouts  119 us (9%)
  other arithmetic  69.5 us (5%)
  blocking collectives  26.6 us (2%)
  starting transfers between devices  19.2 us (2%)
  between operations  14.9 us (1%)
    psum x1, waiting for transfers between devices, local(): lax.psum(dense_part.astype(jnp.bfloat16), 'tensor').astype(jnp.float32)  220 us
    psum x1, waiting for transfers between devices, local(): lax.psum(arrived_grad.astype(jnp.bfloat16), 'tensor').astype(jnp.float32)  220 us
    psum x1, waiting for transfers between devices, local(): attn_full = lax.psum(attn_part, 'tensor')  153 us
    psum x1, waiting for transfers between devices, local(): lax.psum(project_in_grad.astype(jnp.bfloat16), 'expert').astype(jnp.float32)  65.5 us
    psum x1, waiting for transfers between devices, local(): lax.psum(normed_part.astype(jnp.bfloat16), 'tensor').astype(jnp.float32)  47.4 us
    all_to_all x1, waiting for transfers between devices, send_home(): lax.all_to_all(buffer.astype(jnp.bfloat16), 'expert', split_axis=1, conca...  44.4 us
    all_to_all x1, waiting for transfers between devices, send_grads_home(): lax.all_to_all(buffer.astype(jnp.bfloat16), 'expert', split_axis=1, conca...  44.2 us
    all_to_all x1, waiting for transfers between devices, local(): lax.all_to_all(to_slots(mid_low), 'expert', split_axis=0, concat_axis=1,...  38.5 us
  transfers between devices with their start and end apart: 9, of which 9 were waited for; matrix products, arithmetic and copies ran while one was open for 7% of the time, Pallas kernels for 0%

commit v1 on v0

--- a/solution.py
+++ b/solution.py
@@ -312,7 +312,9 @@
         lax.psum(second_gain_grad.astype(jnp.bfloat16), "expert").astype(jnp.float32),
         lax.psum(second_shift_grad.astype(jnp.bfloat16), "expert").astype(jnp.float32),
         lax.psum(project_out_grad.astype(jnp.bfloat16), "expert").astype(jnp.float32),
-        lax.psum(project_in_grad.astype(jnp.bfloat16), "expert").astype(jnp.float32),
+        jnp.sum(lax.all_gather(project_in_grad.astype(jnp.bfloat16), "expert"), axis=0).astype(
+            jnp.float32
+        ),
         lax.psum(first_gain_grad.astype(jnp.bfloat16), "expert").astype(jnp.float32),
         lax.psum(first_shift_grad.astype(jnp.bfloat16), "expert").astype(jnp.float32),
     )

time: 1280 us -> 1330 us (1.039)
  waiting for transfers between devices: 869 us -> 919 us
    all_gather x0 -> x1, waiting for transfers between devices: none -> 65 us  [local(): lax.all_gather(project_in_grad.astype(jnp.bfloat16), 'expert')]
    psum x1, waiting for transfers between devices: 65.5 us -> 48.2 us  [local(): lax.psum(project_out_grad.astype(jnp.bfloat16), 'expert')]
  transfers between devices with their start and end apart: 9 -> 10, of which waited for: 9 -> 10; matrix products, arithmetic and copies ran while one was open for 7% -> 7% of each run, Pallas kernels for 0% -> 0%
where the time goes in v1:
time: 1330 us; the launch traced here: 1320 us
  waiting for transfers between devices  919 us (69%)
  matrix products  140 us (11%)
  local copies, waits for them, and re-layouts  119 us (9%)
  other arithmetic  76.4 us (6%)
  blocking collectives  26.3 us (2%)
  starting transfers between devices  18.6 us (1%)
  between operations  15.4 us (1%)
    psum x1, waiting for transfers between devices, local(): lax.psum(dense_part.astype(jnp.bfloat16), 'tensor').astype(jnp.float32)  220 us
    psum x1, waiting for transfers between devices, local(): lax.psum(arrived_grad.astype(jnp.bfloat16), 'tensor').astype(jnp.float32)  220 us
    psum x1, waiting for transfers between devices, local(): attn_full = lax.psum(attn_part, 'tensor')  153 us
    all_gather x1, waiting for transfers between devices, local(): lax.all_gather(project_in_grad.astype(jnp.bfloat16), 'expert')  65 us
    psum x1, waiting for transfers between devices, local(): lax.psum(project_out_grad.astype(jnp.bfloat16), 'expert')  48.2 us
    psum x1, waiting for transfers between devices, local(): lax.psum(normed_part.astype(jnp.bfloat16), 'tensor').astype(jnp.float32)  47.2 us
    all_to_all x1, waiting for transfers between devices, send_grads_home(): lax.all_to_all(buffer.astype(jnp.bfloat16), 'expert', split_axis=1, conca...  46.1 us
    all_to_all x1, waiting for transfers between devices, send_home(): lax.all_to_all(buffer.astype(jnp.bfloat16), 'expert', split_axis=1, conca...  44.4 us
  transfers between devices with their start and end apart: 10, of which 10 were waited for; matrix products, arithmetic and copies ran while one was open for 7% of the time, Pallas kernels for 0%

profile of v1, /device:TPU:0, one launch (start us, length us, event | category | flops | bytes accessed | tf_op | source)
XLA Modules:
  0.0 1324.9 jit_solution(3342364887834271914)
XLA Ops:
  16.1 23.0 %while.43 = (s32[]{:T(128)}, bf16[2,512,4,64]{1,3,2,0:T(8,128)(2,1)}, f32[2,4,512]{2,1,0:T(4,128)S(1)}, s32[2]{0:T(128)S(1)}, bf16[1024,4,64]{0,2,1:T(8,128)(2,1...) while((s32[]{:T(128)}, ...), condition=%wide.region_5.6_spmd, body=%wide.region_2.5_spmd.sunk | while | flops 562690560 | bytes 35197428 | solution.py:55
  23.7 3.0 fusion.171
  35.2 3.0 fusion.171
  41.9 3.8 fusion.104
  46.4 4.5 scatter_custom_fusion
  50.9 152.7 %all-reduce.10.cloned.1.call-done = f32[1024,1024]{1,0:T(8,128)} async-done(((f32[1024,1024]{1,0:T(8,128)}), f32[1024,1024]{1,0:T(8,128)}) %all-reduce.10.cloned.1.call-update) | async-done | bytes 4194320 | tf_op jit(solution)/shard_map/psum | solution.py:168
  203.6 3.3 fusion.99
  211.6 12.8 gather_fusion
  224.4 3.8 broadcast_select_fusion.1
  228.2 4.6 all-to-all-start
  232.8 4.5 fusion.105
  239.4 4.0 convolution_convert_fusion.5
  243.3 38.5 %all-to-all-done = bf16[16,128,1024]{2,1,0:T(8,128)(2,1)} async-done(((bf16[16,128,1024]{2,1,0:T(8,128)(2,1)}), bf16[16,128,1024]{2,1,0:T(8,128)(2,1)}, u32[]{:S(2)}, u32[]{:S(2)}) %all-to-all-start) | async-done | bytes 4194336 | tf_op jit(solution)/shard_map/all_to_all | solution.py:205
  281.9 2.8 copy.54
  286.7 4.5 fusion.106
  291.2 3.2 copy-done.89
  294.4 6.8 convolution_convert_fusion.1
  301.3 220.2 %all-reduce.18.cloned.1.call-done = (bf16[1024,1024]{1,0:T(8,128)(2,1)}, bf16[2,1024,1024]{2,1,0:T(8,128)(2,1)}) async-done(((bf16[1024,1024]{1,0:T(8,128)(2,1)}, bf16[2,1024,1024]{2,1,0:T(8,128)(2,1)}), (bf16[1024,1024]{1,0:T(8,128)(2,1)}, bf16[2,1024,1024]{2,1,0:T(8,128)(2,1)})) %all-reduce.18.cloned.1.call-update) | async-done | bytes 6291472 | tf_op jit(solution)/shard_map/psum | solution.py:217
  521.5 8.5 copy.55
  530.0 4.7 all-to-all-start.1
  539.4 44.4 %all-to-all-done.1 = bf16[2,1024,1024]{2,0,1:T(2,128)(2,1)} async-done(((bf16[2,1024,1024]{2,0,1:T(2,128)(2,1)}), bf16[2,1024,1024]{2,0,1:T(2,128)(2,1)}, u32[]{:S(2)}, u32[]{:S(2)}) %all-to-all-start.1) | async-done | bytes 4194336 | tf_op jit(solution)/shard_map/all_to_all | solution.py:122
  583.8 7.1 copy.56
  591.0 9.7 gather_fusion.1
  600.7 4.5 fusion.68
  607.1 12.8 gather_fusion.2
  619.8 3.8 broadcast_select_fusion
  623.7 4.6 all-to-all-start.2
  628.3 7.7 fusion.62
  637.3 3.7 convolution_convert_fusion.4
  641.0 36.3 %all-to-all-done.2 = bf16[16,128,1024]{2,1,0:T(8,128)(2,1)} async-done(((bf16[16,128,1024]{2,1,0:T(8,128)(2,1)}), bf16[16,128,1024]{2,1,0:T(8,128)(2,1)}, u32[]{:S(2)}, u32[]{:S(2)}) %all-to-all-start.2) | async-done | bytes 4194336 | tf_op jit(solution)/shard_map/all_to_all | solution.py:249
  677.3 2.8 copy.57
  680.8 12.1 fusion.43
  694.9 6.2 convolution_convert_fusion
  701.1 220.1 %all-reduce.16.cloned.1.call-done = (bf16[2,1024,1024]{2,1,0:T(8,128)(2,1)}, bf16[1024,1024]{1,0:T(8,128)(2,1)}) async-done(((bf16[2,1024,1024]{2,1,0:T(8,128)(2,1)}, bf16[1024,1024]{1,0:T(8,128)(2,1)}), (bf16[2,1024,1024]{2,1,0:T(8,128)(2,1)}, bf16[1024,1024]{1,0:T(8,128)(2,1)})) %all-reduce.16.cloned.1.call-update) | async-done | bytes 6291472 | tf_op jit(solution)/shard_map/psum | solution.py:267
  921.3 8.5 copy.58
  929.8 4.6 all-to-all-start.3
  934.6 2.8 fusion.95
  937.3 46.1 %all-to-all-done.3 = bf16[2,1024,1024]{2,0,1:T(2,128)(2,1)} async-done(((bf16[2,1024,1024]{2,0,1:T(2,128)(2,1)}), bf16[2,1024,1024]{2,0,1:T(2,128)(2,1)}, u32[]{:S(2)}, u32[]{:S(2)}) %all-to-all-start.3) | async-done | bytes 4194336 | tf_op jit(solution)/shard_map/all_to_all | solution.py:128
  983.5 7.1 copy.59
  990.6 9.8 gather_fusion.3
  1000.5 7.5 multiply_reduce_fusion.1
  1008.8 3.6 fusion.98
  1016.8 31.3 %while.44 = (s32[]{:T(128)}, f32[1024,4,64]{0,2,1:T(8,128)S(1)}, f32[1024,4,64]{0,2,1:T(8,128)}, bf16[2,512,4,64]{1,3,2,0:T(8,128)(2,1)}, s32[2]{0:T(128)S(1)}, ...) while((s32[]{:T(128)}, f32[1024,4,64]{0,2,1:T(8,128)S(1)}, ...), condition=%wide.region_27.30_spmd.clone, body=%wide.region_25.29_spmd.clone.sunk | while | flops 1375599104 | bytes 87093672 | solution.py:102
  1022.0 2.6 fusion.183
  1024.5 3.2 multiply_reduce_fusion.6
  1037.5 2.6 fusion.183
  1040.1 3.2 multiply_reduce_fusion.6
  1053.1 5.1 bitcast_convert_fusion
  1058.3 5.5 convolution_convert_fusion.3
  1063.8 4.4 convolution_convert_fusion.2
  1069.9 5.0 convolution_convert_fusion.6
  1077.2 9.5 fusion.107
  1086.8 7.7 fusion.97
  1094.4 47.2 %all-reduce.12.cloned.1.call-done = bf16[1024,1024]{1,0:T(8,128)(2,1)} async-done(((bf16[1024,1024]{1,0:T(8,128)(2,1)}), bf16[1024,1024]{1,0:T(8,128)(2,1)}) %all-reduce.12.cloned.1.call-update) | async-done | bytes 2097168 | tf_op jit(solution)/shard_map/psum | solution.py:293
  1143.6 2.7 fusion.64
  1146.4 2.7 fusion.55
  1149.1 26.3 %all-reduce = (bf16[1024]{0:T(1024)(128)(2,1)S(1)}, bf16[1024]{0:T(1024)(128)(2,1)S(1)}, bf16[1024]{0:T(1024)(128)(2,1)S(1)}, bf16[1024]{0:T(1024)(128)(2,1)S(1)...) all-reduce(bf16[1024]{0:T(1024)(128)(2,1)S(1)} %get-tuple-element.3, ...), channel_id=1, replica_groups=mesh['expert'=8,'tensor'=4] {'expert'}, use_global_device_ids=true, to_apply=%region_32.35 | all-reduce | flops 22528 | bytes 90112 | tf_op jit(solution)/shard_map/psum | solution.py:318
  1179.0 5.4 add_convert_fusion
  1184.4 48.2 %all-reduce.14.cloned.1.call-done = (bf16[256,1024]{1,0:T(8,128)(2,1)}, bf16[1024,1024]{1,0:T(8,128)(2,1)}, bf16[1024,1024]{1,0:T(8,128)(2,1)}) async-done(((bf16[256,1024]{1,0:T(8,128)(2,1)}, bf16[1024,1024]{1,0:T(8,128)(2,1)}, bf16[1024,1024]{1,0:T(8,128)(2,1)}), (bf16[256,1024]{1,0:T(8,128)(2,1)}, bf16[1024,1024]{1,0:T(8,128)(2,1)}, bf16[1024,1024]{1,0:T(8,128)(2,1)})) %all-reduce.14.cloned.1.call-update) | async-done | bytes 4718608 | tf_op jit(solution)/shard_map/psum | solution.py:314
  1234.9 4.1 convert_element_type.244
  1239.0 2.5 convert_element_type.246
  1241.4 65.0 %all-gather.3.cloned.1.call-done = bf16[8192,3,256]{2,0,1:T(8,128)(2,1)} async-done(((bf16[1024,3,256]{2,0,1:T(8,128)(2,1)}), bf16[8192,3,256]{2,0,1:T(8,128)(2,1)}) %all-gather.3.cloned.1.call-update) | async-done | bytes 12582928 | tf_op jit(solution)/shard_map/all_gather | solution.py:315
  1306.5 8.0 reduce_sum.274
  1314.5 3.3 convert_element_type.232
  (306 shorter events, 79.0 us)
Async XLA Ops:
  7.2 232.2 %copy-start = (bf16[1024,1024]{1,0:T(8,128)(2,1)S(1)}, bf16[1024,1024]{1,0:T(8,128)(2,1)}, u32[]{:S(2)}) copy-start(bf16[1024,1024]{1,0:T(8,128)(2,1)} %param.37) | copy-start | bytes 6291460
  7.2 5.8 copy-start.62
  7.2 5.7 copy-start.85
  7.2 196.4 %all-reduce.10.cloned.1.call-start = ((), (), s32[]{:S(2)}) async-start(), calls=%async_computation.4 | async-start | bytes 8388608 | tf_op jit(solution)/shard_map/psum | solution.py:168
  7.3 5.7 copy-start.7
  7.3 5.7 copy-start.84
  9.4 5.8 copy-start.44
  39.0 6.6 copy-start.3
  39.0 6.6 copy-start.9
  39.0 6.6 copy-start.50
  206.9 2.6 copy-start.60
  206.9 2.6 copy-start.77
  228.2 53.7 %all-to-all-start = ((bf16[16,128,1024]{2,1,0:T(8,128)(2,1)}), bf16[16,128,1024]{2,1,0:T(8,128)(2,1)}, u32[]{:S(2)}, u32[]{:S(2)}) async-start(bf16[16,128,1024]{2,1,0:T(8,128)(2,1)} %bitcast.149), calls=%async_computation | async-start | bytes 8388608 | tf_op jit(solution)/shard_map/all_to_all | solution.py:205
  232.8 288.7 %all-reduce.18.cloned.1.call-start = ((), (), s32[]{:S(2)}) async-start(), calls=%async_computation.9 | async-start | bytes 12582912 | tf_op jit(solution)/shard_map/psum | solution.py:217
  281.9 4.8 copy-start.81
  286.7 7.7 copy-start.79
  291.2 3.2 copy-start.89
  530.0 4.7 copy-start.74
  530.0 7.1 copy-start.43
  530.0 53.8 %all-to-all-start.1 = ((bf16[2,1024,1024]{2,0,1:T(2,128)(2,1)}), bf16[2,1024,1024]{2,0,1:T(2,128)(2,1)}, u32[]{:S(2)}, u32[]{:S(2)}) async-start(bf16[2,1024,1024]{2,0,1:T(2,128)(2,1)} %copy.55), calls=%async_computation.1 | async-start | bytes 8388608 | tf_op jit(solution)/shard_map/all_to_all | solution.py:122
  539.4 395.2 %copy-start.30 = (f32[1024,16]{0,1:T(8,128)}, f32[1024,16]{0,1:T(8,128)S(1)}, u32[]{:S(2)}) copy-start(f32[1024,16]{0,1:T(8,128)S(1)} %get-tuple-element.419) | copy-start | bytes 196612
  539.4 395.1 %copy-start.46 = (f32[1024]{0:T(1024)}, f32[1024]{0:T(1024)S(1)}, u32[]{:S(2)}) copy-start(f32[1024]{0:T(1024)S(1)} %get-tuple-element.418) | copy-start | bytes 12292
  539.4 395.1 %copy-start.48 = (f32[1024]{0:T(1024)}, f32[1024]{0:T(1024)S(1)}, u32[]{:S(2)}) copy-start(f32[1024]{0:T(1024)S(1)} %fusion.85) | copy-start | bytes 12292
  600.7 4.6 copy-start.13
  605.2 329.3 %copy-start.56 = (f32[1024]{0:T(1024)}, f32[1024]{0:T(1024)S(1)}, u32[]{:S(2)}) copy-start(f32[1024]{0:T(1024)S(1)} %mul.424) | copy-start | bytes 12292
  623.7 53.7 %all-to-all-start.2 = ((bf16[16,128,1024]{2,1,0:T(8,128)(2,1)}), bf16[16,128,1024]{2,1,0:T(8,128)(2,1)}, u32[]{:S(2)}, u32[]{:S(2)}) async-start(bf16[16,128,1024]{2,1,0:T(8,128)(2,1)} %bitcast.148), calls=%async_computation.2 | async-start | bytes 8388608 | tf_op jit(solution)/shard_map/all_to_all | solution.py:249
  628.2 293.0 %all-reduce.16.cloned.1.call-start = ((), (), s32[]{:S(2)}) async-start(), calls=%async_computation.8 | async-start | bytes 12582912 | tf_op jit(solution)/shard_map/psum | solution.py:267
  628.3 9.0 copy-start.83
  677.3 3.4 copy-start.80
  680.2 12.7 copy-start.22
  680.8 14.1 %copy-start.82 = (bf16[2,1024,1024]{2,1,0:T(8,128)(2,1)S(1)}, bf16[2,1024,1024]{2,1,0:T(8,128)(2,1)}, u32[]{:S(2)}) copy-start(bf16[2,1024,1024]{2,1,0:T(8,128)(2,1)} %param.38) | copy-start | bytes 12582916
  929.8 53.7 %all-to-all-start.3 = ((bf16[2,1024,1024]{2,0,1:T(2,128)(2,1)}), bf16[2,1024,1024]{2,0,1:T(2,128)(2,1)}, u32[]{:S(2)}, u32[]{:S(2)}) async-start(bf16[2,1024,1024]{2,0,1:T(2,128)(2,1)} %copy.58), calls=%async_computation.3 | async-start | bytes 8388608 | tf_op jit(solution)/shard_map/all_to_all | solution.py:128
  934.4 207.2 %all-reduce.12.cloned.1.call-start = ((), (), s32[]{:S(2)}) async-start(), calls=%async_computation.5 | async-start | bytes 4194304 | tf_op jit(solution)/shard_map/psum | solution.py:293
  934.5 56.1 %copy-start.68 = (f32[1024]{0:T(1024)}, f32[1024]{0:T(1024)S(1)}, u32[]{:S(2)}) copy-start(f32[1024]{0:T(1024)S(1)} %neg.18) | copy-start | bytes 12292
  990.6 9.9 copy-start.53
  990.6 9.9 copy-start.55
  990.6 9.9 copy-start.61
  1000.4 7.6 copy-start.73
  1000.5 7.6 copy-start.6
  1000.5 7.7 copy-start.11
  1000.5 8.3 copy-start.19
  1008.8 4.3 copy-start.14
  1024.5 3.2 copy-start.33
  1040.1 3.2 copy-start.33
  1048.1 4.7 copy-start.34
  1053.1 5.1 copy-start.40
  1053.1 5.2 copy-start.2
  1058.2 174.4 %all-reduce.14.cloned.1.call-start = ((), (), s32[]{:S(2)}) async-start(), calls=%async_computation.7 | async-start | bytes 9437184 | tf_op jit(solution)/shard_map/psum | solution.py:314
  1058.3 5.5 copy-start.15
  1058.3 5.5 copy-start.88
  1063.8 4.4 copy-start.25
  1063.8 4.4 copy-start.29
  1069.8 236.7 %all-gather.3.cloned.1.call-start = ((), (), s32[]{:S(2)}) async-start(), calls=%async_computation.6 | async-start | bytes 14155776 | tf_op jit(solution)/shard_map/all_gather | solution.py:315
  1075.0 11.8 slice-start
  1077.2 9.6 copy-start.23
  1077.2 9.6 slice-start.1
  1086.8 56.8 %copy-start.8 = (bf16[1024,1024]{1,0:T(8,128)(2,1)S(1)}, bf16[1024,1024]{1,0:T(8,128)(2,1)}, u32[]{:S(2)}) copy-start(bf16[1024,1024]{1,0:T(8,128)(2,1)} %param.24) | copy-start | bytes 6291460
  1094.4 51.9 %copy-start.71 = (f32[1024]{0:T(1024)S(1)}, f32[1024]{0:T(1024)}, u32[]{:S(2)}) copy-start(f32[1024]{0:T(1024)} %copy-done.70) | copy-start | bytes 12292
  1143.6 2.8 copy-start.16
  1143.6 5.5 copy-start.75
  1143.6 5.5 copy-start.76
  1143.6 35.4 %copy-start.67 = (f32[1024]{0:T(1024)S(1)}, f32[1024]{0:T(1024)}, u32[]{:S(2)}) copy-start(f32[1024]{0:T(1024)} %copy-done.66) | copy-start | bytes 12292
  1232.6 6.3 copy-start.27
  1306.5 11.3 copy-start.1
  (48 other events, 70.1 us)
Sparse Core Ops, SparseCore 0:
  45.8 157.6 all-reduce.9
  301.4 220.0 all-reduce.17
  701.2 219.9 all-reduce.15
  1058.3 83.2 all-reduce.11
  1145.6 86.9 all-reduce.13
  1234.4 72.0 all-gather.2
